TPU v7x, 128 devices: a whole 4x4x4 slice. The times are simulated.
128 devices in a mesh: row: 8 (over x, core), col: 16 (over z, y).
Axes of the slice: x: 4, y: 4, z: 4, core: 2. Of those that a mesh axis runs over, the one named last changes fastest.
Arguments:
- density_tiles: float32 [3, 4096, 4096], P(None, ('row', 'col')), may hold values from -0.012 to 0.012
- tile_ids: int32 [4096], P(('row', 'col')), may hold values from 0 to 16383, as said below
- batch_blocks: int32 [128, 8], replicated, may hold values from 0 to 127, as said below
- basis_values: float32 [128, 512, 1024], P(('row', 'col')), may hold values from -6 to 6
- grid_weight: float32 [128, 1024], P(('row', 'col')), may hold values from 0.0002 to 0.002
- xc_kernel: float32 [128, 1024], P(('row', 'col')), may hold values from -2 to -0.5
- grid_coord: float32 [3, 128, 1024], P(None, ('row', 'col')), may hold values from -1 to 1
- orbitals: float32 [8192, 512], P('row'), may hold values from -1.5 to 1.5
- precond_diag: float32 [8192], P('row'), may hold values from 1 to 4
- orbital_energy: float32 [512], replicated, may hold values from -3 to -0.5
Outputs:
- new_density: float32 [3, 4096, 4096], P(None, ('row', 'col'))
Inputs may be any that keep to these rules, and one draw needn't show every extreme that they name: `tile_ids`: the 32 slots of device (r, c), counted in row+col order, list distinct tiles I * 128 + J with I in the r-th range of 16 blocks and J in the c-th range of 8 blocks. `batch_blocks`: each row holds 8 ascending blocks, no two in the same range of 8 blocks, and exactly 1 of them in each range of 16 blocks.
All inputs are finite; a program needn't handle non-finite values.
Results may differ from a plain program's by a relative error of at most 0.0003.
Values sent between devices are 32-bit elements; how exact they have to be, the bound alone decides.
A program may use at most 128 MiB of HBM per device.

v0:
```python
import jax
import jax.numpy as jnp
from jax import lax
from jax.sharding import PartitionSpec as P

NB = 8192
TILE = 64
FB = 8
PRECISE = lax.Precision.HIGHEST


def from_root(value, axis, source):
    kept = jnp.where(lax.axis_index(axis) == source, value, 0).astype(value.dtype)
    return lax.psum(kept, axis)


def slot_plan(blocks, owner_row, owner_col, col_blocks, per_range):
    matched = blocks // col_blocks == owner_col[..., None]
    active = jnp.any(matched, axis=-1)
    positions = jnp.arange(blocks.shape[-1], dtype=jnp.int32)
    column_place = jnp.sum(jnp.where(matched, positions, 0), axis=-1)
    row_place = owner_row[..., None] * per_range + jnp.arange(per_range, dtype=jnp.int32)
    return (active, row_place, column_place)


def local(
    density_tiles,
    tile_ids,
    batch_blocks,
    basis_values,
    grid_weight,
    xc_kernel,
    grid_coord,
    orbitals,
    precond_diag,
    orbital_energy,
):
    row_count = lax.axis_size("row")
    col_count = lax.axis_size("col")
    device_count = row_count * col_count
    own_row = lax.axis_index("row")
    own_col = lax.axis_index("col")
    own_index = own_row * col_count + own_col
    block_count = NB // TILE
    row_blocks = block_count // row_count
    col_blocks = block_count // col_count
    per_range = FB // row_count
    batch_count = basis_values.shape[0]
    slot_count = batch_count * per_range
    tile_area = TILE * TILE
    tile_local = tile_ids.shape[0]
    orbital_count = orbitals.shape[1]
    col_ratio = col_count // row_count
    col_width = col_blocks * TILE
    batch_width = FB * TILE
    orbital_piece = lax.dynamic_slice_in_dim(
        orbitals, own_col % col_ratio * col_width, col_width, 0
    )
    orbital_cols = from_root(orbital_piece, "row", own_col // col_ratio)
    requests = batch_blocks.reshape(device_count, batch_count, FB)
    owner_rows = jnp.full((device_count, batch_count), own_row, dtype=jnp.int32)
    owner_cols = jnp.full((device_count, batch_count), own_col, dtype=jnp.int32)
    active, row_place, column_place = slot_plan(
        requests, owner_rows, owner_cols, col_blocks, per_range
    )
    want_rows = jnp.take_along_axis(requests, row_place, axis=2)
    want_col = jnp.take_along_axis(requests, column_place[..., None], axis=2)
    wanted = jnp.where(active[..., None], want_rows * block_count + want_col, -1).reshape(-1)
    selector = (wanted[:, None] == tile_ids[None, :]).astype(jnp.float32)
    outgoing = jnp.einsum("ns,dsx->dnx", selector, density_tiles, precision=PRECISE)
    arrived = lax.all_to_all(outgoing, ("row", "col"), split_axis=1, concat_axis=1, tiled=True)
    own_blocks = lax.dynamic_slice_in_dim(requests, own_index, 1, 0)[0]
    block_pos = jnp.arange(FB, dtype=jnp.int32)
    batch_pos = jnp.arange(batch_count, dtype=jnp.int32)
    source = (block_pos // per_range)[None, :, None] * col_count + (own_blocks // col_blocks)[
        :, None, :
    ]
    lookup = (
        source * slot_count
        + batch_pos[:, None, None] * per_range
        + (block_pos % per_range)[None, :, None]
    )
    density = jnp.take(arrived, lookup.reshape(-1), axis=1).reshape(
        3, batch_count, FB, FB, TILE, TILE
    )
    density = density.transpose(0, 1, 2, 4, 3, 5).reshape(3, batch_count, batch_width, batch_width)
    projected = jnp.einsum("dkmn,knp->dkmp", density, basis_values, precision=PRECISE)
    response = jnp.sum(basis_values[None] * projected, axis=2)
    potential = xc_kernel[None] * response + grid_coord
    weighted = basis_values[None] * (grid_weight[None] * potential)[:, :, None, :]
    hamiltonian = jnp.einsum("dkmp,knp->dkmn", weighted, basis_values, precision=PRECISE)
    ham_tiles = (
        hamiltonian.reshape(3, batch_count, FB, TILE, FB, TILE)
        .transpose(0, 1, 2, 4, 3, 5)
        .reshape(3, batch_count * FB * FB, tile_area)
    )
    owners = jnp.arange(device_count, dtype=jnp.int32)
    target_rows = (owners // col_count)[:, None]
    target_cols = (owners % col_count)[:, None]
    mine_all = jnp.broadcast_to(own_blocks[None], (device_count, batch_count, FB))
    back_active, back_rows, back_col = slot_plan(
        mine_all, target_rows, target_cols, col_blocks, per_range
    )
    pick_index = (batch_pos[None, :, None] * FB + back_rows) * FB + back_col[..., None]
    keep_mask = back_active[..., None].reshape(-1)
    returning = jnp.where(
        keep_mask[None, :, None], jnp.take(ham_tiles, pick_index.reshape(-1), axis=1), 0.0
    )
    returned = lax.all_to_all(returning, ("row", "col"), split_axis=1, concat_axis=1, tiled=True)
    ham_listed = jnp.einsum("ns,dnx->dsx", selector, returned, precision=PRECISE)
    local_rows = tile_ids // block_count - own_row * row_blocks
    local_cols = tile_ids % block_count - own_col * col_blocks
    row_hot = (local_rows[None, :] == jnp.arange(row_blocks, dtype=jnp.int32)[:, None]).astype(
        jnp.float32
    )
    col_hot = (local_cols[None, :] == jnp.arange(col_blocks, dtype=jnp.int32)[:, None]).astype(
        jnp.float32
    )
    block_matrix = jnp.einsum(
        "rs,cs,dsab->dracb",
        row_hot,
        col_hot,
        ham_listed.reshape(3, tile_local, TILE, TILE),
        precision=PRECISE,
    )
    block_matrix = block_matrix.reshape(3, row_blocks * TILE, col_width)
    partial_rows = jnp.einsum("drc,co->dro", block_matrix, orbital_cols, precision=PRECISE)
    summed_rows = lax.psum(partial_rows, "col")
    response_orbs = -summed_rows / (precond_diag[:, None] - orbital_energy[None, :])
    response_piece = lax.dynamic_slice_in_dim(
        response_orbs, own_col % col_ratio * col_width, col_width, 1
    )
    response_cols = from_root(response_piece, "row", own_col // col_ratio)
    x_rows = jnp.take(response_orbs.reshape(3, row_blocks, TILE, orbital_count), local_rows, axis=1)
    c_rows = jnp.take(orbitals.reshape(row_blocks, TILE, orbital_count), local_rows, axis=0)
    x_cols = jnp.take(response_cols.reshape(3, col_blocks, TILE, orbital_count), local_cols, axis=1)
    c_cols = jnp.take(orbital_cols.reshape(col_blocks, TILE, orbital_count), local_cols, axis=0)
    renewed = jnp.einsum("dsao,sbo->dsab", x_rows, c_cols, precision=PRECISE)
    renewed = renewed + jnp.einsum("sao,dsbo->dsab", c_rows, x_cols, precision=PRECISE)
    return renewed.reshape(3, tile_local, tile_area)


def solution(mesh):
    placed = (
        P(None, ("row", "col"), None),
        P(("row", "col")),
        P(),
        P(("row", "col"), None, None),
        P(("row", "col"), None),
        P(("row", "col"), None),
        P(None, ("row", "col"), None),
        P("row", None),
        P("row"),
        P(),
    )
    return jax.shard_map(
        local, mesh=mesh, in_specs=placed, out_specs=P(None, ("row", "col"), None), check_vma=False
    )
```

profile of v0, /device:TPU:0, one launch (start us, length us, event | category | flops | bytes accessed | tf_op | source)
XLA Modules:
  0.0 686.3 jit_solution(637120942322534087)
XLA Ops:
  15.5 7.5 %copy.47 = f32[3,128,4096]{2,0,1:T(4,128)} copy(f32[3,128,4096]{2,1,0:T(8,128)S(1)} %convolution_bitcast_fusion) | data formatting | bytes 12582912 | tf_op jit(solution)/shard_map/ns,dsx->dnx/transpose | solution.py:70
  23.1 12.2 %all-to-all-start = ((f32[3,128,4096]{2,0,1:T(4,128)}), f32[3,128,4096]{2,0,1:T(4,128)}, u32[]{:S(2)}, u32[]{:S(2)}) async-start(f32[3,128,4096]{2,0,1:T(4,128)} %copy.47), calls=%async_computation | async-start | bytes 16777216 | tf_op jit(solution)/shard_map/all_to_all | solution.py:71
  35.7 103.5 %all-to-all-done = f32[3,128,4096]{2,0,1:T(4,128)} async-done(((f32[3,128,4096]{2,0,1:T(4,128)}), f32[3,128,4096]{2,0,1:T(4,128)}, u32[]{:S(2)}, u32[]{:S(2)}) %all-to-all-start) | async-done | bytes 6291488 | tf_op jit(solution)/shard_map/all_to_all | solution.py:71
  139.2 8.1 %gather_fusion.1 = f32[64,3,4096]{2,1,0:T(4,128)} fusion(f32[3,128,4096]{2,0,1:T(4,128)} %all-to-all-done, s32[1024]{0:T(1024)S(1)} %pad_clamp_fusion.2), kind=kCustom, calls=%fused_computation.3 | custom fusion | bytes 6291712 | tf_op jit(solution)/shard_map/jit(_take)/gather | solution.py:83
  147.3 5.7 copy.48
  153.0 6.1 gather.31
  159.1 3.7 select_bitcast_fusion.1
  162.8 8.1 %copy.49 = f32[3,1,8,64,8,64]{5,4,3,2,0,1:T(8,128)} copy(f32[3,1,8,64,8,64]{5,3,4,2,0,1:T(8,128)S(1)} %select_bitcast_fusion.1) | data formatting | bytes 6291456 | tf_op jit(solution)/shard_map/transpose | solution.py:86
  170.9 6.4 reshape.542
  177.3 13.6 %fusion.6 = f32[3,1024]{1,0:T(4,128)S(1)} fusion(f32[512,1024]{1,0:T(8,128)} %bitcast.155, f32[3,512,512]{2,1,0:T(8,128)} %reshape.542, f32[1,512,1024]{2,1,0:T(8,128)} %param.15), kind=kOutput, calls=%fused_computation.16 | convolution fusion | flops 9666819072 | bytes 7352320 | tf_op jit(solution)/shard_map/dkmn,knp->dkmp/dot_general | solution.py:87
  191.0 11.9 %fusion.32 = f32[3,1,512,512]{3,2,0,1:T(8,128)} fusion(f32[1,512,1024]{2,1,0:T(8,128)S(1)} %copy-done.12, f32[3,1024]{1,0:T(4,128)S(1)} %bitcast.152, f32[512,1024]{1,0:T(8,128)S(1)} %bitcast.156), kind=kOutput, calls=%fused_computation.47 | convolution fusion | flops 9665249280 | bytes 7352320 | tf_op jit(solution)/shard_map/dkmp,knp->dkmn/dot_general | solution.py:91
  202.9 5.8 reshape.543
  208.7 6.6 copy.70
  215.3 5.9 reshape.544
  221.1 6.0 copy.51
  227.1 11.9 %gather_fusion.2 = f32[128,3,4096]{2,1,0:T(4,128)} fusion(f32[3,64,4096]{2,0,1:T(4,128)} %copy.51, s32[1024]{0:T(1024)S(1)} %pad_clamp_fusion.1), kind=kCustom, calls=%fused_computation.4 | custom fusion | bytes 12583424 | tf_op jit(solution)/shard_map/jit(_take)/gather | solution.py:107
  239.1 11.6 %select_bitcast_fusion = f32[3,128,4096]{2,0,1:T(4,128)} fusion(f32[128,3,4096]{2,1,0:T(4,128)} %gather_fusion.2, pred[128]{0:T(512)(128)(4,1)S(1)} %fusion.61, pred[128]{0:T(512)(128)(4,1)S(1)} %compare_and_fusion), kind=kLoop, calls=%fused_computation.14 | loop fusion | flops 3145728 | bytes 12583168 | tf_op jit(solution)/shard_map/jit(_where)/select_n | solution.py:106
  250.7 8.1 %all-to-all-start.1 = ((f32[3,128,4096]{2,0,1:T(4,128)}), f32[3,128,4096]{2,0,1:T(4,128)}, u32[]{:S(2)}, u32[]{:S(2)}) async-start(f32[3,128,4096]{2,0,1:T(4,128)} %select_bitcast_fusion), calls=%async_computation.1 | async-start | bytes 16777216 | tf_op jit(solution)/shard_map/all_to_all | solution.py:109
  261.3 107.4 %all-to-all-done.1 = f32[3,128,4096]{2,0,1:T(4,128)} async-done(((f32[3,128,4096]{2,0,1:T(4,128)}), f32[3,128,4096]{2,0,1:T(4,128)}, u32[]{:S(2)}, u32[]{:S(2)}) %all-to-all-start.1) | async-done | bytes 6291488 | tf_op jit(solution)/shard_map/all_to_all | solution.py:109
  368.7 8.8 %fusion.15 = f32[3,32,4096]{2,1,0:T(8,128)S(1)} fusion(f32[3,128,4096]{2,0,1:T(4,128)} %all-to-all-done.1, s32[128]{0:T(128)S(1)} %fusion.77, s32[32]{0:T(128)S(1)} %copy-done.7), kind=kOutput, calls=%fused_computation.29 | convolution fusion | flops 603983872 | bytes 7864960 | tf_op jit(solution)/shard_map/ns,dnx->dsx/dot_general | solution.py:110
  380.0 15.5 %convolution_bitcast_fusion.1 = f32[3,16,64,8,64]{4,1,2,0,3:T(8,128)} fusion(f32[3,32,64,64]{3,2,1,0:T(8,128)} %reshape.545, f32[32,16]{0,1:T(8,128)S(1)} %convert_bitcast_fusion, f32[32,8]{0,1:T(8,128)S(1)} %convert_bitcast_fusion.1), kind=kOutput, calls=%fused_computation.30 | convolution fusion | flops 603983872 | bytes 7867392 | tf_op jit(solution)/shard_map/rs,cs,dsab->dracb/dot_general | solution.py:119
  395.5 16.3 %copy.54 = f32[3,16,64,8,64]{4,3,2,1,0:T(8,128)} copy(f32[3,16,64,8,64]{4,1,2,0,3:T(8,128)} %convolution_bitcast_fusion.1) | data formatting | bytes 12582912 | tf_op jit(solution)/shard_map/rs,cs,dsab->dracb/transpose | solution.py:119
  411.8 11.5 %reshape.546 = f32[3,1024,512]{2,1,0:T(8,128)} reshape(f32[3,16,64,8,64]{4,3,2,1,0:T(8,128)} %copy.54) | data formatting | bytes 12582912 | tf_op jit(solution)/shard_map/reshape | solution.py:126
  423.3 13.5 %fusion.41 = f32[3,1024,512]{2,1,0:T(8,128)} fusion(f32[3,1024,512]{2,1,0:T(8,128)} %reshape.546, f32[512,512]{1,0:T(8,128)} %all-reduce.4.cloned.1.call-done), kind=kOutput, calls=%fused_computation.48 | convolution fusion | flops 9663676416 | bytes 13631488 | tf_op jit(solution)/shard_map/drc,co->dro/dot_general | solution.py:127
  439.1 117.3 %all-reduce.6.cloned.1.call-done = f32[3,1024,512]{2,1,0:T(8,128)} async-done(((f32[3,1024,512]{2,1,0:T(8,128)}), f32[3,1024,512]{2,1,0:T(8,128)}) %all-reduce.6.cloned.1.call-update) | async-done | bytes 6291472 | tf_op jit(solution)/shard_map/psum | solution.py:128
  556.4 4.5 negate_divide_fusion
  565.6 4.4 gather_fusion.5
  572.8 8.9 %gather_fusion.3 = f32[32,3,64,512]{3,2,1,0:T(8,128)} fusion(f32[3,16,64,512]{3,2,1,0:T(8,128)} %bitcast.146, s32[1024]{0:T(1024)S(1)} %pad_clamp_fusion), kind=kCustom, calls=%fused_computation.5 | custom fusion | bytes 25165952 | tf_op jit(solution)/shard_map/jit(_take)/gather | solution.py:134
  581.7 52.6 %all-reduce.8.cloned.1.call-done = f32[3,8,64,512]{3,2,1,0:T(8,128)} async-done(((f32[3,8,64,512]{3,2,1,0:T(8,128)}), f32[3,8,64,512]{3,2,1,0:T(8,128)}) %all-reduce.8.cloned.1.call-update) | async-done | bytes 3145744 | tf_op jit(solution)/shard_map/psum | solution.py:14
  634.3 7.7 %gather_fusion.4 = f32[32,3,64,512]{3,2,1,0:T(8,128)} fusion(f32[3,8,64,512]{3,2,1,0:T(8,128)} %all-reduce.8.cloned.1.call-done, s32[1024]{0:T(1024)S(1)} %pad_clamp_fusion.3), kind=kCustom, calls=%fused_computation.6 | custom fusion | bytes 25165952 | tf_op jit(solution)/shard_map/jit(_take)/gather | solution.py:136
  642.0 15.3 %fusion = f32[32,3,64,64]{3,2,1,0:T(8,128)S(1)} fusion(f32[32,3,64,512]{3,2,1,0:T(8,128)} %gather_fusion.4, pred[32]{0:T(512)(128)(4,1)S(1)} %get-tuple-element.10, f32[32,64,512]{2,1,0:T(8,128)} %gather_fusion.5, pred[32]{0:T(512)(128)(4,1)S(1)} %get-tuple-element.16), kind=kOutput, calls=%fused_computation.8 | convolution fusion | flops 2420113408 | bytes 18350144 | tf_op jit(solution)/shard_map/sao,dsbo->dsab/dot_general | solution.py:139
  657.4 15.4 %bitcast_add_fusion = f32[3,32,64,64]{2,3,0,1:T(8,128)} fusion(f32[32,3,64,64]{3,2,1,0:T(8,128)S(1)} %fusion, f32[32,3,64,512]{3,2,1,0:T(8,128)S(1)} %copy-done.3, pred[32]{0:T(512)(128)(4,1)S(1)} %get-tuple-element.16, f32[32,64,512]{2,1,0:T(8,128)S(1)} %copy-done.5, pred[32]{0:T(512)(128)(4,1)S(1)} %get-tuple-element.10), kind=kOutput, calls=%fused_computation.35 | convolution fusion | flops 2420506624 | bytes 19923008 | tf_op jit(solution)/shard_map/dsao,sbo->dsab/dot_general | solution.py:138
  (77 shorter events, 30.8 us)
Async XLA Ops:
  6.5 5.6 copy-start
  23.1 116.1 %all-to-all-start = ((f32[3,128,4096]{2,0,1:T(4,128)}), f32[3,128,4096]{2,0,1:T(4,128)}, u32[]{:S(2)}, u32[]{:S(2)}) async-start(f32[3,128,4096]{2,0,1:T(4,128)} %copy.47), calls=%async_computation | async-start | bytes 16777216 | tf_op jit(solution)/shard_map/all_to_all | solution.py:71
  177.3 13.6 %copy-start.6 = (f32[3,1,1024]{2,1,0:T(1,128)S(1)}, f32[3,1,1024]{2,1,0:T(1,128)}, u32[]{:S(2)}) copy-start(f32[3,1,1024]{2,1,0:T(1,128)} %param.18) | copy-start | bytes 36868
  177.3 13.6 %copy-start.9 = (f32[1,1024]{1,0:T(1,128)S(1)}, f32[1,1024]{1,0:T(1,128)}, u32[]{:S(2)}) copy-start(f32[1,1024]{1,0:T(1,128)} %param.17) | copy-start | bytes 12292
  177.3 13.6 %copy-start.10 = (f32[1,1024]{1,0:T(1,128)S(1)}, f32[1,1024]{1,0:T(1,128)}, u32[]{:S(2)}) copy-start(f32[1,1024]{1,0:T(1,128)} %param.16) | copy-start | bytes 12292
  177.3 13.7 %copy-start.12 = (f32[1,512,1024]{2,1,0:T(8,128)S(1)}, f32[1,512,1024]{2,1,0:T(8,128)}, u32[]{:S(2)}) copy-start(f32[1,512,1024]{2,1,0:T(8,128)} %param.15) | copy-start | bytes 6291460
  250.7 10.6 %copy-start.7 = (s32[32]{0:T(128)S(1)}, s32[32]{0:T(128)}, u32[]{:S(2)}) copy-start(s32[32]{0:T(128)} %param.13) | copy-start | bytes 388
  250.7 118.0 %all-to-all-start.1 = ((f32[3,128,4096]{2,0,1:T(4,128)}), f32[3,128,4096]{2,0,1:T(4,128)}, u32[]{:S(2)}, u32[]{:S(2)}) async-start(f32[3,128,4096]{2,0,1:T(4,128)} %select_bitcast_fusion), calls=%async_computation.1 | async-start | bytes 16777216 | tf_op jit(solution)/shard_map/all_to_all | solution.py:109
  258.8 164.5 %all-reduce.4.cloned.1.call-start = ((), (), s32[]{:S(2)}) async-start(), calls=%async_computation.2 | async-start | bytes 2097152 | tf_op jit(solution)/shard_map/psum | solution.py:14
  261.2 295.2 %all-reduce.6.cloned.1.call-start = ((), (), s32[]{:S(2)}) async-start(), calls=%async_computation.3 | async-start | bytes 12582912 | tf_op jit(solution)/shard_map/psum | solution.py:128
  436.9 0.7 copy-start.8
  436.9 0.7 copy-start.11
  436.9 197.4 %all-reduce.8.cloned.1.call-start = ((), (), s32[]{:S(2)}) async-start(), calls=%async_computation.4 | async-start | bytes 6291456 | tf_op jit(solution)/shard_map/psum | solution.py:14
  560.9 2.6 copy-start.2
  565.6 4.5 copy-start.4
  642.0 15.3 %copy-start.3 = (f32[32,3,64,512]{3,2,1,0:T(8,128)S(1)}, f32[32,3,64,512]{3,2,1,0:T(8,128)}, u32[]{:S(2)}) copy-start(f32[32,3,64,512]{3,2,1,0:T(8,128)} %gather_fusion.3) | copy-start | bytes 37748740
  642.0 15.3 %copy-start.5 = (f32[32,64,512]{2,1,0:T(8,128)S(1)}, f32[32,64,512]{2,1,0:T(8,128)}, u32[]{:S(2)}) copy-start(f32[32,64,512]{2,1,0:T(8,128)} %gather_fusion) | copy-start | bytes 12582916
  657.3 22.2 %copy-start.1 = (f32[3,32,4096]{2,1,0:T(8,128)S(1)}, f32[3,32,4096]{2,1,0:T(8,128)}, u32[]{:S(2)}) copy-start(f32[3,32,4096]{2,1,0:T(8,128)} %param.12) | copy-start | bytes 4718596
Sparse Core Ops, SparseCore 0:
  262.0 87.8 all-reduce.3
  437.0 119.3 all-reduce.5
  565.7 68.6 all-reduce.7
where the time goes:
time: 694 us; the launch traced here: 686 us
  waiting for transfers between devices  381 us (55%)
  local copies, waits for them, and re-layouts  146 us (21%)
  matrix products  97.3 us (14%)
  other arithmetic  27.9 us (4%)
  starting transfers between devices  20.8 us (3%)
  between operations  13.6 us (2%)
    psum x1, waiting for transfers between devices, local(): summed_rows = lax.psum(partial_rows, 'col')  117 us
    all_to_all x1, waiting for transfers between devices, local(): lax.all_to_all(returning, ('row', 'col'), split_axis=1, concat_axis=1, ti...  107 us
    all_to_all x1, waiting for transfers between devices, local(): lax.all_to_all(outgoing, ('row', 'col'), split_axis=1, concat_axis=1, til...  103 us
    psum x2, waiting for transfers between devices, from_root(): return lax.psum(kept, axis)  52.6 us
    gather x3, local copies, waits for them, and re-layouts, local(): jnp.take(arrived, lookup.reshape(-1), axis=1)  19.9 us
    transpose x1, local copies, waits for them, and re-layouts, local(): jnp.einsum('rs,cs,dsab->dracb', row_hot, col_hot, ham_listed.reshape(3, t...  16.3 us
    dot_general x1, matrix products, local(): jnp.einsum('rs,cs,dsab->dracb', row_hot, col_hot, ham_listed.reshape(3, t...  15.5 us
    dot_general x1, matrix products, local(): renewed = jnp.einsum('dsao,sbo->dsab', x_rows, c_cols, precision=PRECISE)  15.4 us
  transfers between devices with their start and end apart: 5, of which 4 were waited for; matrix products, arithmetic and copies ran while one was open for 11% of the time, Pallas kernels for 0%

commit v1 on v0

--- a/solution.py
+++ b/solution.py
@@ -125,7 +125,10 @@
     )
     block_matrix = block_matrix.reshape(3, row_blocks * TILE, col_width)
     partial_rows = jnp.einsum("drc,co->dro", block_matrix, orbital_cols, precision=PRECISE)
-    summed_rows = lax.psum(partial_rows, "col")
+    peers, summed_rows = (lax.axis_size("col"), partial_rows)
+    for far in [1 << k for k in range(peers.bit_length() - 1)]:
+        swap = [(i, i ^ far) for i in range(peers)]
+        summed_rows = summed_rows + lax.ppermute(summed_rows, "col", swap)
     response_orbs = -summed_rows / (precond_diag[:, None] - orbital_energy[None, :])
     response_piece = lax.dynamic_slice_in_dim(
         response_orbs, own_col % col_ratio * col_width, col_width, 1

time: 694 us -> 1140 us (1.64)
  waiting for transfers between devices: 381 us -> 799 us
  other arithmetic: 27.9 us -> 41.8 us
    ppermute x0 -> x4, waiting for transfers between devices: none -> 535 us  [local(): summed_rows = summed_rows + lax.ppermute(summed_rows, 'col', swap)]
    psum x1 -> x0, waiting for transfers between devices: 117 us -> none  [local(): summed_rows = lax.psum(partial_rows, 'col')]
    add x0 -> x3, other arithmetic: none -> 13 us  [local(): summed_rows = summed_rows + lax.ppermute(summed_rows, 'col', swap)]
    ppermute x0 -> x4, starting transfers between devices: none -> 11.8 us  [local(): summed_rows = summed_rows + lax.ppermute(summed_rows, 'col', swap)]
  transfers between devices with their start and end apart: 5 -> 8, of which waited for: 4 -> 7; matrix products, arithmetic and copies ran while one was open for 11% -> 7% of each run, Pallas kernels for 0% -> 0%
where the time goes in v1:
time: 1140 us; the launch traced here: 1130 us
  waiting for transfers between devices  799 us (70%)
  local copies, waits for them, and re-layouts  145 us (13%)
  matrix products  97.4 us (9%)
  other arithmetic  41.8 us (4%)
  starting transfers between devices  31.9 us (3%)
  between operations  14 us (1%)
    ppermute x4, waiting for transfers between devices, local(): summed_rows = summed_rows + lax.ppermute(summed_rows, 'col', swap)  535 us
    all_to_all x1, waiting for transfers between devices, local(): lax.all_to_all(returning, ('row', 'col'), split_axis=1, concat_axis=1, ti...  107 us
    all_to_all x1, waiting for transfers between devices, local(): lax.all_to_all(outgoing, ('row', 'col'), split_axis=1, concat_axis=1, til...  103 us
    psum x2, waiting for transfers between devices, from_root(): return lax.psum(kept, axis)  52.2 us
  transfers between devices with their start and end apart: 8, of which 7 were waited for; matrix products, arithmetic and copies ran while one was open for 7% of the time, Pallas kernels for 0%

profile of v1, /device:TPU:0, one launch (start us, length us, event | category | flops | bytes accessed | tf_op | source)
XLA Modules:
  0.0 1129.2 jit_solution(2764481185531145050)
XLA Ops:
  15.5 7.5 copy.47
  23.1 11.9 %all-to-all-start = ((f32[3,128,4096]{2,0,1:T(4,128)}), f32[3,128,4096]{2,0,1:T(4,128)}, u32[]{:S(2)}, u32[]{:S(2)}) async-start(f32[3,128,4096]{2,0,1:T(4,128)} %copy.47), calls=%async_computation | async-start | bytes 16777216 | tf_op jit(solution)/shard_map/all_to_all | solution.py:71
  35.4 103.5 %all-to-all-done = f32[3,128,4096]{2,0,1:T(4,128)} async-done(((f32[3,128,4096]{2,0,1:T(4,128)}), f32[3,128,4096]{2,0,1:T(4,128)}, u32[]{:S(2)}, u32[]{:S(2)}) %all-to-all-start) | async-done | bytes 6291488 | tf_op jit(solution)/shard_map/all_to_all | solution.py:71
  138.9 8.1 gather_fusion.1
  152.7 6.1 gather.31
  162.5 8.1 copy.49
  170.6 6.5 reshape.542
  177.1 13.6 %fusion.6 = f32[3,1024]{1,0:T(4,128)S(1)} fusion(f32[512,1024]{1,0:T(8,128)} %bitcast.155, f32[3,512,512]{2,1,0:T(8,128)} %reshape.542, f32[1,512,1024]{2,1,0:T(8,128)} %param.15), kind=kOutput, calls=%fused_computation.16 | convolution fusion | flops 9666819072 | bytes 7352320 | tf_op jit(solution)/shard_map/dkmn,knp->dkmp/dot_general | solution.py:87
  190.7 11.9 %fusion.32 = f32[3,1,512,512]{3,2,0,1:T(8,128)} fusion(f32[1,512,1024]{2,1,0:T(8,128)S(1)} %copy-done.13, f32[3,1024]{1,0:T(4,128)S(1)} %bitcast.152, f32[512,1024]{1,0:T(8,128)S(1)} %bitcast.156), kind=kOutput, calls=%fused_computation.47 | convolution fusion | flops 9665249280 | bytes 7352320 | tf_op jit(solution)/shard_map/dkmp,knp->dkmn/dot_general | solution.py:91
  202.6 6.0 reshape.543
  208.6 6.6 copy.70
  215.2 5.9 reshape.544
  221.0 6.0 copy.51
  227.0 11.7 %gather_fusion.2 = f32[128,3,4096]{2,1,0:T(4,128)} fusion(f32[3,64,4096]{2,0,1:T(4,128)} %copy.51, s32[1024]{0:T(1024)S(1)} %pad_clamp_fusion.1), kind=kCustom, calls=%fused_computation.4 | custom fusion | bytes 12583424 | tf_op jit(solution)/shard_map/jit(_take)/gather | solution.py:107
  238.7 11.6 %select_bitcast_fusion = f32[3,128,4096]{2,0,1:T(4,128)} fusion(f32[128,3,4096]{2,1,0:T(4,128)} %gather_fusion.2, pred[128]{0:T(512)(128)(4,1)S(1)} %fusion.61, pred[128]{0:T(512)(128)(4,1)S(1)} %compare_and_fusion), kind=kLoop, calls=%fused_computation.14 | loop fusion | flops 3145728 | bytes 12583168 | tf_op jit(solution)/shard_map/jit(_where)/select_n | solution.py:106
  250.4 8.1 all-to-all-start.1
  261.0 107.4 %all-to-all-done.1 = f32[3,128,4096]{2,0,1:T(4,128)} async-done(((f32[3,128,4096]{2,0,1:T(4,128)}), f32[3,128,4096]{2,0,1:T(4,128)}, u32[]{:S(2)}, u32[]{:S(2)}) %all-to-all-start.1) | async-done | bytes 6291488 | tf_op jit(solution)/shard_map/all_to_all | solution.py:109
  368.4 8.8 fusion.15
  379.7 15.5 %convolution_bitcast_fusion.1 = f32[3,16,64,8,64]{4,1,2,0,3:T(8,128)} fusion(f32[3,32,64,64]{3,2,1,0:T(8,128)} %reshape.545, f32[32,16]{0,1:T(8,128)S(1)} %convert_bitcast_fusion, f32[32,8]{0,1:T(8,128)S(1)} %convert_bitcast_fusion.1), kind=kOutput, calls=%fused_computation.30 | convolution fusion | flops 603983872 | bytes 7867392 | tf_op jit(solution)/shard_map/rs,cs,dsab->dracb/dot_general | solution.py:119
  395.2 16.3 %copy.54 = f32[3,16,64,8,64]{4,3,2,1,0:T(8,128)} copy(f32[3,16,64,8,64]{4,1,2,0,3:T(8,128)} %convolution_bitcast_fusion.1) | data formatting | bytes 12582912 | tf_op jit(solution)/shard_map/rs,cs,dsab->dracb/transpose | solution.py:119
  411.5 11.5 %reshape.546 = f32[3,1024,512]{2,1,0:T(8,128)} reshape(f32[3,16,64,8,64]{4,3,2,1,0:T(8,128)} %copy.54) | data formatting | bytes 12582912 | tf_op jit(solution)/shard_map/reshape | solution.py:126
  423.0 13.6 %fusion.41 = f32[3,1024,512]{2,1,0:T(8,128)S(1)} fusion(f32[3,1024,512]{2,1,0:T(8,128)} %reshape.546, f32[512,512]{1,0:T(8,128)} %all-reduce.3.cloned.1.call-done), kind=kOutput, calls=%fused_computation.48 | convolution fusion | flops 9663676416 | bytes 13631488 | tf_op jit(solution)/shard_map/drc,co->dro/dot_general | solution.py:127
  437.1 133.3 %collective-permute-done = f32[3,1024,512]{2,1,0:T(8,128)} collective-permute-done((f32[3,1024,512]{2,1,0:T(8,128)S(1)}, f32[3,1024,512]{2,1,0:T(8,128)}, u32[]{:S(2)}, u32[]{:S(2)}) %collective-permute-start) | collective-permute-done | bytes 6291488 | tf_op jit(solution)/shard_map/ppermute | solution.py:131
  576.1 133.1 %collective-permute-done.1 = f32[3,1024,512]{2,1,0:T(8,128)} collective-permute-done((f32[3,1024,512]{2,1,0:T(8,128)S(1)}, f32[3,1024,512]{2,1,0:T(8,128)}, u32[]{:S(2)}, u32[]{:S(2)}) %collective-permute-start.1) | collective-permute-done | bytes 6291488 | tf_op jit(solution)/shard_map/ppermute | solution.py:131
  717.8 134.9 %collective-permute-done.2 = f32[3,1024,512]{2,1,0:T(8,128)} collective-permute-done((f32[3,1024,512]{2,1,0:T(8,128)S(1)}, f32[3,1024,512]{2,1,0:T(8,128)}, u32[]{:S(2)}, u32[]{:S(2)}) %collective-permute-start.2) | collective-permute-done | bytes 6291488 | tf_op jit(solution)/shard_map/ppermute | solution.py:131
  863.0 134.2 %collective-permute-done.3 = f32[3,1024,512]{2,1,0:T(8,128)} collective-permute-done((f32[3,1024,512]{2,1,0:T(8,128)S(1)}, f32[3,1024,512]{2,1,0:T(8,128)}, u32[]{:S(2)}, u32[]{:S(2)}) %collective-permute-start.3) | collective-permute-done | bytes 6291488 | tf_op jit(solution)/shard_map/ppermute | solution.py:131
  997.2 6.6 negate_divide_fusion
  1015.9 8.7 gather_fusion.3
  1024.6 52.2 %all-reduce.5.cloned.1.call-done = f32[3,8,64,512]{3,2,1,0:T(8,128)} async-done(((f32[3,8,64,512]{3,2,1,0:T(8,128)}), f32[3,8,64,512]{3,2,1,0:T(8,128)}) %all-reduce.5.cloned.1.call-update) | async-done | bytes 3145744 | tf_op jit(solution)/shard_map/psum | solution.py:14
  1076.8 7.7 gather_fusion.4
  1084.5 15.3 %fusion = f32[32,3,64,64]{3,2,1,0:T(8,128)S(1)} fusion(f32[32,3,64,512]{3,2,1,0:T(8,128)} %gather_fusion.4, pred[32]{0:T(512)(128)(4,1)S(1)} %get-tuple-element.10, f32[32,64,512]{2,1,0:T(8,128)} %gather_fusion.5, pred[32]{0:T(512)(128)(4,1)S(1)} %get-tuple-element.16), kind=kOutput, calls=%fused_computation.8 | convolution fusion | flops 2420113408 | bytes 18350144 | tf_op jit(solution)/shard_map/sao,dsbo->dsab/dot_general | solution.py:142
  1099.9 15.4 %bitcast_add_fusion = f32[3,32,64,64]{2,3,0,1:T(8,128)} fusion(f32[32,3,64,64]{3,2,1,0:T(8,128)S(1)} %fusion, f32[32,3,64,512]{3,2,1,0:T(8,128)S(1)} %copy-done.3, pred[32]{0:T(512)(128)(4,1)S(1)} %get-tuple-element.16, f32[32,64,512]{2,1,0:T(8,128)S(1)} %copy-done.6, pred[32]{0:T(512)(128)(4,1)S(1)} %get-tuple-element.10), kind=kOutput, calls=%fused_computation.35 | convolution fusion | flops 2420506624 | bytes 19923008 | tf_op jit(solution)/shard_map/dsao,sbo->dsab/dot_general | solution.py:141
  (87 shorter events, 67.5 us)
Async XLA Ops:
  6.5 5.6 copy-start
  23.1 115.8 %all-to-all-start = ((f32[3,128,4096]{2,0,1:T(4,128)}), f32[3,128,4096]{2,0,1:T(4,128)}, u32[]{:S(2)}, u32[]{:S(2)}) async-start(f32[3,128,4096]{2,0,1:T(4,128)} %copy.47), calls=%async_computation | async-start | bytes 16777216 | tf_op jit(solution)/shard_map/all_to_all | solution.py:71
  177.1 13.6 %copy-start.7 = (f32[3,1,1024]{2,1,0:T(1,128)S(1)}, f32[3,1,1024]{2,1,0:T(1,128)}, u32[]{:S(2)}) copy-start(f32[3,1,1024]{2,1,0:T(1,128)} %param.18) | copy-start | bytes 36868
  177.1 13.6 %copy-start.10 = (f32[1,1024]{1,0:T(1,128)S(1)}, f32[1,1024]{1,0:T(1,128)}, u32[]{:S(2)}) copy-start(f32[1,1024]{1,0:T(1,128)} %param.17) | copy-start | bytes 12292
  177.1 13.6 %copy-start.11 = (f32[1,1024]{1,0:T(1,128)S(1)}, f32[1,1024]{1,0:T(1,128)}, u32[]{:S(2)}) copy-start(f32[1,1024]{1,0:T(1,128)} %param.16) | copy-start | bytes 12292
  177.1 13.6 %copy-start.13 = (f32[1,512,1024]{2,1,0:T(8,128)S(1)}, f32[1,512,1024]{2,1,0:T(8,128)}, u32[]{:S(2)}) copy-start(f32[1,512,1024]{2,1,0:T(8,128)} %param.15) | copy-start | bytes 6291460
  250.4 10.6 copy-start.8
  250.4 118.0 %all-to-all-start.1 = ((f32[3,128,4096]{2,0,1:T(4,128)}), f32[3,128,4096]{2,0,1:T(4,128)}, u32[]{:S(2)}, u32[]{:S(2)}) async-start(f32[3,128,4096]{2,0,1:T(4,128)} %select_bitcast_fusion), calls=%async_computation.1 | async-start | bytes 16777216 | tf_op jit(solution)/shard_map/all_to_all | solution.py:109
  258.5 164.6 %all-reduce.3.cloned.1.call-start = ((), (), s32[]{:S(2)}) async-start(), calls=%async_computation.2 | async-start | bytes 2097152 | tf_op jit(solution)/shard_map/psum | solution.py:14
  260.9 815.9 %all-reduce.5.cloned.1.call-start = ((), (), s32[]{:S(2)}) async-start(), calls=%async_computation.3 | async-start | bytes 6291456 | tf_op jit(solution)/shard_map/psum | solution.py:14
  436.6 133.8 %collective-permute-start = (f32[3,1024,512]{2,1,0:T(8,128)S(1)}, f32[3,1024,512]{2,1,0:T(8,128)}, u32[]{:S(2)}, u32[]{:S(2)}) collective-permute-start(f32[3,1024,512]{2,1,0:T(8,128)S(1)} %fusion.41), channel_id=1, source_target_pairs={{0,1},{1,0},{2,3},{3,2},{4,5},{5,4},{6,7},{7,6},{8,9},{9,8},{10,11... | collective-permute-start | bytes 18874376 | tf_op jit(solution)/shard_map/ppermute | solution.py:131
  574.7 134.4 %collective-permute-start.1 = (f32[3,1024,512]{2,1,0:T(8,128)S(1)}, f32[3,1024,512]{2,1,0:T(8,128)}, u32[]{:S(2)}, u32[]{:S(2)}) collective-permute-start(f32[3,1024,512]{2,1,0:T(8,128)S(1)} %add.247), channel_id=1, source_target_pairs={{0,2},{1,3},{2,0},{3,1},{4,6},{5,7},{6,4},{7,5},{8,10},{9,11},{10,... | collective-permute-start | bytes 18874376 | tf_op jit(solution)/shard_map/ppermute | solution.py:131
  713.5 149.2 %copy-start.9 = (f32[1024]{0:T(1024)S(1)}, f32[1024]{0:T(1024)}, u32[]{:S(2)}) copy-start(f32[1024]{0:T(1024)} %param.20) | copy-start | bytes 12292
  713.5 149.2 %copy-start.12 = (f32[512]{0:T(512)S(1)}, f32[512]{0:T(512)}, u32[]{:S(2)}) copy-start(f32[512]{0:T(512)} %param.21) | copy-start | bytes 6148
  713.5 139.2 %collective-permute-start.2 = (f32[3,1024,512]{2,1,0:T(8,128)S(1)}, f32[3,1024,512]{2,1,0:T(8,128)}, u32[]{:S(2)}, u32[]{:S(2)}) collective-permute-start(f32[3,1024,512]{2,1,0:T(8,128)S(1)} %add.248), channel_id=1, source_target_pairs={{0,4},{1,5},{2,6},{3,7},{4,0},{5,1},{6,2},{7,3},{8,12},{9,13},{10,... | collective-permute-start | bytes 18874376 | tf_op jit(solution)/shard_map/ppermute | solution.py:131
  857.1 5.9 copy-start.5
  857.1 140.1 %collective-permute-start.3 = (f32[3,1024,512]{2,1,0:T(8,128)S(1)}, f32[3,1024,512]{2,1,0:T(8,128)}, u32[]{:S(2)}, u32[]{:S(2)}) collective-permute-start(f32[3,1024,512]{2,1,0:T(8,128)S(1)} %add.249), channel_id=1, source_target_pairs={{0,8},{1,9},{2,10},{3,11},{4,12},{5,13},{6,14},{7,15},{8,0},{9,1},... | collective-permute-start | bytes 18874376 | tf_op jit(solution)/shard_map/ppermute | solution.py:131
  1003.8 2.6 copy-start.2
  1008.6 4.4 copy-start.4
  1084.5 15.3 %copy-start.3 = (f32[32,3,64,512]{3,2,1,0:T(8,128)S(1)}, f32[32,3,64,512]{3,2,1,0:T(8,128)}, u32[]{:S(2)}) copy-start(f32[32,3,64,512]{3,2,1,0:T(8,128)} %gather_fusion.3) | copy-start | bytes 37748740
  1084.5 15.3 %copy-start.6 = (f32[32,64,512]{2,1,0:T(8,128)S(1)}, f32[32,64,512]{2,1,0:T(8,128)}, u32[]{:S(2)}) copy-start(f32[32,64,512]{2,1,0:T(8,128)} %gather_fusion) | copy-start | bytes 12582916
  1099.8 22.2 %copy-start.1 = (f32[3,32,4096]{2,1,0:T(8,128)S(1)}, f32[3,32,4096]{2,1,0:T(8,128)}, u32[]{:S(2)}) copy-start(f32[3,32,4096]{2,1,0:T(8,128)} %param.12) | copy-start | bytes 4718596
Sparse Core Ops, SparseCore 0:
  261.6 87.8 all-reduce.2
  1008.7 67.9 all-reduce.4
